TPU v7x, 128 devices: a whole 4x4x4 slice. The times are simulated.
128 devices in a mesh: seq: 32 (over y, x, core), dp: 4 (over z).
Axes of the slice: x: 4, y: 4, z: 4, core: 2. Of those that a mesh axis runs over, the one named last changes fastest.
Arguments:
- features: bfloat16 [4, 8192, 512], P('dp', 'seq'), may hold values from -6 to 6
- curve_pos: int32 [4, 8192], P('dp'), may hold values from 0 to 8191, as said below
- pattern: int32 [4, 64, 8], P('dp'), may hold values from 0 to 63, as said below
- ln1_gain: float32 [512], replicated, may hold values from 0.5 to 1.5
- w_qkv: bfloat16 [512, 1536], replicated, may hold values from -1 to 1
- w_out: bfloat16 [512, 512], replicated, may hold values from -0.25 to 0.25
- ln2_gain: float32 [512], replicated, may hold values from 0.5 to 1.5
- w_up: bfloat16 [512, 2048], replicated, may hold values from -0.25 to 0.25
- w_down: bfloat16 [2048, 512], replicated, may hold values from -0.125 to 0.125
- out_grad: bfloat16 [4, 8192, 512], P('dp', 'seq'), may hold values from -6 to 6
Outputs:
- block_out: bfloat16 [4, 8192, 512], P('dp', 'seq')
- input_grad: bfloat16 [4, 8192, 512], P('dp', 'seq')
- grad_qkv: float32 [512, 1536], replicated
- grad_out: float32 [512, 512], replicated
- grad_up: float32 [512, 2048], replicated
- grad_down: float32 [2048, 512], replicated
- grad_gain1: float32 [512], replicated
- grad_gain2: float32 [512], replicated
Inputs may be any that keep to these rules, and one draw needn't show every extreme that they name: `curve_pos`: for each tile a permutation of the 8192 curve positions. Of the 256 nodes of one aligned block, at most 16 have positions in one aligned block of 256 curve positions, and in every tile some node block sends exactly 16 to some curve block. `pattern`: each list holds 8 distinct blocks: first the query block q itself, then blocks (q + 2**j) or (q - 2**j) modulo 64.
All inputs are finite; a program needn't handle non-finite values.
Results may differ from a plain program's by a relative error of at most 0.018.
Values may be sent and summed in bfloat16 or wider, within the bound.
A program may use at most 128 MiB of HBM per device.

v0:
```python
from functools import partial
import jax
import jax.numpy as jnp
from jax import lax
from jax.sharding import PartitionSpec as P

D = 512
HEADS = 8
BLK = 128
EPSILON = 1e-05


def from_behind(x, axis, by):
    length = lax.axis_size(axis)
    return lax.ppermute(x, axis, [(i, (i + by) % length) for i in range(length)])


def layer_norm(rows_in, gain_vec):
    values = rows_in.astype(jnp.float32)
    centered = values - jnp.mean(values, axis=-1, keepdims=True)
    inverse = lax.rsqrt(jnp.mean(centered * centered, axis=-1, keepdims=True) + EPSILON)
    normed = centered * inverse
    return ((normed * gain_vec).astype(jnp.bfloat16), normed, inverse)


def norm_back(incoming, gain_vec, normed, inverse):
    scaled = incoming * gain_vec
    return inverse * (
        scaled
        - jnp.mean(scaled, axis=-1, keepdims=True)
        - normed * jnp.mean(scaled * normed, axis=-1, keepdims=True)
    )


def gelu_back(pre_act, incoming):
    return jax.vjp(partial(jax.nn.gelu, approximate=True), pre_act)[1](incoming)[0]


def inner_rows(left_mat, right_mat):
    return lax.dot_general(
        left_mat, right_mat, (((0,), (0,)), ((), ())), preferred_element_type=jnp.float32
    )


def times_transposed(left_mat, right_mat):
    return lax.dot_general(
        left_mat, right_mat, (((1,), (1,)), ((), ())), preferred_element_type=jnp.float32
    )


def split_heads(rows_in):
    return rows_in.reshape(rows_in.shape[0] // BLK, BLK, HEADS, D // HEADS)


def listed_heads(keyval_all, selected):
    blocks = keyval_all.reshape(keyval_all.shape[0] // BLK, BLK, 2 * D)
    picked = blocks[selected]
    shape_out = picked.shape[:3] + (HEADS, D // HEADS)
    return (picked[..., :D].reshape(shape_out), picked[..., D:].reshape(shape_out))


def shift_distances(seq_devices):
    levels = seq_devices.bit_length() - 1
    distances = []
    for level_idx in range(levels):
        stride = 2**level_idx
        if 2 * stride == seq_devices:
            distances.append(stride)
        else:
            distances.extend([stride, -stride])
    return distances


def node_plan(position, seq_index, dev_rows, capacity, seq_devices):
    own_position = lax.dynamic_slice_in_dim(position, seq_index * dev_rows, dev_rows)
    target_dev = own_position // dev_rows
    dest_hits = (target_dev[:, None] == jnp.arange(seq_devices, dtype=jnp.int32)[None, :]).astype(
        jnp.int32
    )
    send_rank = jnp.sum((jnp.cumsum(dest_hits, axis=0) - dest_hits) * dest_hits, axis=1)
    send_index = target_dev * capacity + send_rank
    layout = position.reshape(seq_devices, dev_rows)
    arriving = (layout // dev_rows == seq_index).astype(jnp.int32)
    arrive_rank = jnp.cumsum(arriving, axis=1) - arriving
    source_index = jnp.arange(seq_devices, dtype=jnp.int32)[:, None] * capacity + arrive_rank
    del source_index
    total = position.shape[0]
    wanted = seq_index * dev_rows + jnp.arange(dev_rows, dtype=jnp.int32)
    slot_node = jnp.sum(
        jnp.where(
            position[None, :] == wanted[:, None], jnp.arange(total, dtype=jnp.int32)[None, :], 0
        ),
        axis=1,
    )
    source_for_slot = slot_node // dev_rows * capacity + arrive_rank.reshape(-1)[slot_node]
    return (send_index, source_for_slot)


def attention_forward(queries, keyval_all, selected):
    query_heads = split_heads(queries)
    key_heads, value_heads = listed_heads(keyval_all, selected)
    scores = (
        jnp.einsum("aihd,akjhd->haikj", query_heads, key_heads, preferred_element_type=jnp.float32)
        * 0.125
    )
    largest = jnp.max(scores, axis=(3, 4), keepdims=True)
    totals = jnp.sum(jnp.exp(scores - largest), axis=(3, 4), keepdims=True)
    log_totals = largest + jnp.log(totals)
    attn_probs = jnp.exp(scores - log_totals).astype(jnp.bfloat16)
    result = jnp.einsum(
        "haikj,akjhd->aihd", attn_probs, value_heads, preferred_element_type=jnp.float32
    )
    return (result.astype(jnp.bfloat16).reshape(queries.shape[0], D), log_totals)


def attention_backward(queries, keyval_all, selected, attn_out, log_totals, grad_attn):
    query_heads = split_heads(queries)
    key_heads, value_heads = listed_heads(keyval_all, selected)
    out_heads = split_heads(attn_out)
    grad_heads = split_heads(grad_attn)
    scores = (
        jnp.einsum("aihd,akjhd->haikj", query_heads, key_heads, preferred_element_type=jnp.float32)
        * 0.125
    )
    attn_exact = jnp.exp(scores - log_totals)
    attn_probs = attn_exact.astype(jnp.bfloat16)
    grad_probs = jnp.einsum(
        "aihd,akjhd->haikj", grad_heads, value_heads, preferred_element_type=jnp.float32
    )
    row_dots = jnp.einsum(
        "aihd,aihd->hai", grad_heads, out_heads, preferred_element_type=jnp.float32
    )[..., None, None]
    grad_scores = (attn_exact * (grad_probs - row_dots) * 0.125).astype(jnp.bfloat16)
    grad_query = jnp.einsum(
        "haikj,akjhd->aihd", grad_scores, key_heads, preferred_element_type=jnp.float32
    )
    grad_keys = jnp.einsum(
        "haikj,aihd->akjhd", grad_scores, query_heads, preferred_element_type=jnp.float32
    )
    grad_values = jnp.einsum(
        "haikj,aihd->akjhd", attn_probs, grad_heads, preferred_element_type=jnp.float32
    )
    block_shape = grad_keys.shape[:3] + (D,)
    grad_picked = jnp.concatenate(
        [grad_keys.reshape(block_shape), grad_values.reshape(block_shape)], axis=-1
    )
    total_rows = keyval_all.shape[0]
    grad_keyval = (
        jnp.zeros((total_rows // BLK, BLK, 2 * D), jnp.float32).at[selected].add(grad_picked)
    )
    return (
        grad_query.astype(jnp.bfloat16).reshape(queries.shape[0], D),
        grad_keyval.reshape(total_rows, 2 * D),
    )


def ring_position(kind):
    seq_index = lax.axis_index("seq")
    if kind == "x":
        return seq_index // 2 % 4
    if kind == "y":
        return seq_index // 8
    return lax.axis_index("dp")


def ring_send(rows, kind, shift):
    if kind == "z":
        size = lax.axis_size("dp")
        return lax.ppermute(rows, "dp", [(i, (i + shift) % size) for i in range(size)])
    size = lax.axis_size("seq")
    if kind == "x":
        move = lambda i: i - i // 2 % 4 * 2 + (i // 2 % 4 + shift) % 4 * 2
    else:
        move = lambda i: (i // 8 + shift) % 4 * 8 + i % 8
    return lax.ppermute(rows, "seq", [(i, move(i)) for i in range(size)])


def in_member_order(pieces, position):
    count = len(pieces)
    placed = jnp.zeros((count,) + pieces[0].shape, pieces[0].dtype)
    for offset, piece in enumerate(pieces):
        placed = lax.dynamic_update_index_in_dim(placed, piece, (position - offset) % count, 0)
    return placed


def scatter_stage(rows, gains, kind):
    position = ring_position(kind)
    part = rows.shape[0] // 4
    chunks = rows.reshape(4, part, rows.shape[1])
    total = lax.dynamic_index_in_dim(chunks, position, keepdims=False)
    gains_sent = None if gains is None else gains.astype(jnp.bfloat16)
    gains_got = [gains_sent]
    for shift in (1, 2, 3):
        piece = lax.dynamic_index_in_dim(chunks, (position + shift) % 4, keepdims=False)
        message = piece.astype(jnp.bfloat16)
        if gains is not None:
            message = jnp.concatenate([message, gains_sent], axis=0)
        got = ring_send(message, kind, shift)
        total = total + got[:part].astype(jnp.float32)
        if gains is not None:
            gains_got.append(got[part:])
    if gains is not None:
        canon = in_member_order(gains_got, position).astype(jnp.float32)
        gains = canon[0] + canon[1] + (canon[2] + canon[3])
    return (total, gains)


def gather_stage(rows, kind):
    position = ring_position(kind)
    pieces = [rows] + [ring_send(rows, kind, shift) for shift in (1, 2, 3)]
    canon = in_member_order(pieces, position)
    return canon.reshape(4 * rows.shape[0], rows.shape[1])


AXIS_ORDERS = (("x", "y", "z"),)


def reduce_everywhere(rows, gains):
    seq_devices = lax.axis_size("seq")
    core = lax.axis_index("seq") % 2
    pairs = [(i, i ^ 1) for i in range(seq_devices)]
    half = rows.shape[0] // 2
    halves = rows.reshape(2, half, rows.shape[1])
    own = lax.dynamic_index_in_dim(halves, core, keepdims=False)
    other = lax.dynamic_index_in_dim(halves, 1 - core, keepdims=False)
    gains_sent = gains.astype(jnp.bfloat16)
    got = lax.ppermute(
        jnp.concatenate([other.astype(jnp.bfloat16), gains_sent], axis=0), "seq", pairs
    )
    summed = own + got[:half].astype(jnp.float32)
    gains = gains_sent.astype(jnp.float32) + got[half:].astype(jnp.float32)
    third = half // len(AXIS_ORDERS)
    done = []
    for part_idx, order in enumerate(AXIS_ORDERS):
        part = summed[part_idx * third : (part_idx + 1) * third]
        part_gains = gains if part_idx == 0 else None
        for kind in order:
            part, part_gains = scatter_stage(part, part_gains, kind)
        if part_idx == 0:
            gains = part_gains
        part = part.astype(jnp.bfloat16)
        for kind in reversed(order):
            part = gather_stage(part, kind)
        done.append(part)
    mine = jnp.concatenate(done, axis=0)
    partner = lax.ppermute(mine, "seq", pairs)
    full = in_member_order([mine, partner], core).reshape(rows.shape)
    return (full.astype(jnp.float32), gains)


def on_device(
    features, curve_pos, pattern, ln1_gain, w_qkv, w_out, ln2_gain, w_up, w_down, out_grad
):
    seq_devices = lax.axis_size("seq")
    seq_index = lax.axis_index("seq")
    dev_rows = features.shape[1]
    capacity = 2 * dev_rows // seq_devices
    blocks_dev = dev_rows // BLK
    position = curve_pos[0]
    send_index, source_for_slot = node_plan(position, seq_index, dev_rows, capacity, seq_devices)
    outgoing = jnp.zeros((seq_devices * capacity, D), jnp.bfloat16).at[send_index].set(features[0])
    arrived = lax.all_to_all(
        outgoing.reshape(seq_devices, capacity, D), "seq", split_axis=0, concat_axis=0, tiled=True
    )
    curve_rows = arrived.reshape(seq_devices * capacity, D)[source_for_slot]
    normed_a, normed1, inverse1 = layer_norm(curve_rows, ln1_gain)
    qkv = jnp.dot(normed_a, w_qkv, preferred_element_type=jnp.float32).astype(jnp.bfloat16)
    queries = qkv[:, :D]
    keyval = qkv[:, D:]
    distances = shift_distances(seq_devices)
    pieces = [keyval]
    for distance in distances:
        pieces.append(from_behind(keyval, "seq", distance))
    keyval_all = jnp.concatenate(pieces, axis=0)
    source_dev = jnp.stack(
        [seq_index] + [(seq_index - distance) % seq_devices for distance in distances]
    )
    key_blocks = (
        source_dev[:, None] * blocks_dev + jnp.arange(blocks_dev, dtype=jnp.int32)[None, :]
    ).reshape(-1)
    own_lists = lax.dynamic_slice_in_dim(pattern[0], seq_index * blocks_dev, blocks_dev, axis=0)
    matches = (own_lists[:, :, None] == key_blocks[None, None, :]).astype(jnp.int32)
    selected = jnp.sum(
        matches * jnp.arange(key_blocks.shape[0], dtype=jnp.int32)[None, None, :], axis=-1
    )
    attn_out, log_totals = attention_forward(queries, keyval_all, selected)
    hidden_res = (
        curve_rows.astype(jnp.float32)
        + jnp.dot(attn_out, w_out, preferred_element_type=jnp.float32)
    ).astype(jnp.bfloat16)
    normed_b, normed2, inverse2 = layer_norm(hidden_res, ln2_gain)
    pre_act = jnp.dot(normed_b, w_up, preferred_element_type=jnp.float32)
    activated = jax.nn.gelu(pre_act, approximate=True).astype(jnp.bfloat16)
    curve_out = (
        hidden_res.astype(jnp.float32)
        + jnp.dot(activated, w_down, preferred_element_type=jnp.float32)
    ).astype(jnp.bfloat16)
    leaving = (
        jnp.zeros((seq_devices * capacity, D), jnp.bfloat16).at[source_for_slot].set(curve_out)
    )
    returned = lax.all_to_all(
        leaving.reshape(seq_devices, capacity, D), "seq", split_axis=0, concat_axis=0, tiled=True
    )
    block_out = returned.reshape(seq_devices * capacity, D)[send_index]
    grad_outgoing = (
        jnp.zeros((seq_devices * capacity, D), jnp.bfloat16).at[send_index].set(out_grad[0])
    )
    grad_arrived = lax.all_to_all(
        grad_outgoing.reshape(seq_devices, capacity, D),
        "seq",
        split_axis=0,
        concat_axis=0,
        tiled=True,
    )
    grad_curve = grad_arrived.reshape(seq_devices * capacity, D)[source_for_slot]
    grad_pre = gelu_back(pre_act, times_transposed(grad_curve, w_down)).astype(jnp.bfloat16)
    grad_down = inner_rows(activated, grad_curve)
    grad_normed_b = times_transposed(grad_pre, w_up)
    grad_up = inner_rows(normed_b, grad_pre)
    grad_gain2 = jnp.sum(grad_normed_b * normed2, axis=0)
    grad_up, grad_down = lax.psum((grad_up, grad_down), ("seq", "dp"))
    grad_hidden = (
        grad_curve.astype(jnp.float32) + norm_back(grad_normed_b, ln2_gain, normed2, inverse2)
    ).astype(jnp.bfloat16)
    grad_attn = times_transposed(grad_hidden, w_out).astype(jnp.bfloat16)
    grad_out = inner_rows(attn_out, grad_hidden)
    resent = [keyval]
    for distance in distances:
        resent.append(from_behind(keyval, "seq", distance))
    keyval_back = jnp.concatenate(resent, axis=0)
    grad_query, grad_keyval_all = attention_backward(
        queries, keyval_back, selected, attn_out, log_totals, grad_attn
    )
    grad_keyval = grad_keyval_all[:dev_rows]
    for index_pos, distance in enumerate(distances):
        partial_rows = grad_keyval_all[(index_pos + 1) * dev_rows : (index_pos + 2) * dev_rows]
        grad_keyval = grad_keyval + from_behind(
            partial_rows.astype(jnp.bfloat16), "seq", -distance
        ).astype(partial_rows.dtype)
    grad_qkv_rows = jnp.concatenate([grad_query, grad_keyval.astype(jnp.bfloat16)], axis=1)
    grad_normed_a = times_transposed(grad_qkv_rows, w_qkv)
    grad_qkv = inner_rows(normed_a, grad_qkv_rows)
    grad_gain1 = jnp.sum(grad_normed_a * normed1, axis=0)
    grad_curve_in = (
        grad_hidden.astype(jnp.float32) + norm_back(grad_normed_a, ln1_gain, normed1, inverse1)
    ).astype(jnp.bfloat16)
    grad_leaving = (
        jnp.zeros((seq_devices * capacity, D), jnp.bfloat16).at[source_for_slot].set(grad_curve_in)
    )
    grad_returned = lax.all_to_all(
        grad_leaving.reshape(seq_devices, capacity, D),
        "seq",
        split_axis=0,
        concat_axis=0,
        tiled=True,
    )
    input_grad = grad_returned.reshape(seq_devices * capacity, D)[send_index]
    weight_rows = jnp.concatenate(
        [grad_qkv[:, index * D : (index + 1) * D] for index in range(3)] + [grad_out], axis=0
    )
    gain_rows = jnp.zeros((8, D), jnp.float32).at[0].set(grad_gain1).at[1].set(grad_gain2)
    weight_rows, gain_rows = reduce_everywhere(weight_rows, gain_rows)
    grad_qkv = jnp.concatenate(
        [weight_rows[index * D : (index + 1) * D] for index in range(3)], axis=1
    )
    grad_out = weight_rows[3 * D :]
    grad_gain1 = gain_rows[0]
    grad_gain2 = gain_rows[1]
    return (
        block_out[None],
        input_grad[None],
        grad_qkv,
        grad_out,
        grad_up,
        grad_down,
        grad_gain1,
        grad_gain2,
    )


def solution(mesh):
    return jax.shard_map(
        on_device,
        mesh=mesh,
        in_specs=(
            P("dp", "seq", None),
            P("dp", None),
            P("dp", None, None),
            P(),
            P(),
            P(),
            P(),
            P(),
            P(),
            P("dp", "seq", None),
        ),
        out_specs=(P("dp", "seq", None), P("dp", "seq", None), P(), P(), P(), P(), P(), P()),
        check_vma=False,
    )
```

profile of v0, /device:TPU:1, one launch (start us, length us, event | category | flops | bytes accessed | tf_op | source)
XLA Modules:
  0.0 500.6 jit_solution(13440220894397012022)
XLA Ops:
  14.5 8.6 %all-to-all-start = ((bf16[32,16,512]{2,1,0:T(8,128)(2,1)}), bf16[32,16,512]{2,1,0:T(8,128)(2,1)S(1)}, u32[]{:S(2)}, u32[]{:S(2)}) async-start(bf16[32,16,512]{2,1,0:T(8,128)(2,1)} %bitcast.16), calls=%async_computation | async-start | bytes 1048576 | tf_op jit(solution)/shard_map/all_to_all | solution.py:262
  55.9 5.1 %collective-permute-start.5 = (bf16[256,1024]{1,0:T(8,128)(2,1)}, bf16[256,1024]{1,0:T(8,128)(2,1)S(1)}, u32[]{:S(2)}, u32[]{:S(2)}) collective-permute-start(bf16[256,1024]{1,0:T(8,128)(2,1)} %get-tuple-element.69), channel_id=1, source_target_pairs={{0,112},{4,116},{8,120},{12,124},{16,0},{20,4},{24,8},{28,12},{32,... | collective-permute-start | bytes 1572872 | tf_op jit(solution)/shard_map/ppermute | solution.py:15
  73.9 19.9 %collective-permute-start.8 = (bf16[256,1024]{1,0:T(8,128)(2,1)}, bf16[256,1024]{1,0:T(8,128)(2,1)S(1)}, u32[]{:S(2)}, u32[]{:S(2)}) collective-permute-start(bf16[256,1024]{1,0:T(8,128)(2,1)} %get-tuple-element.69), channel_id=1, source_target_pairs={{0,64},{4,68},{8,72},{12,76},{16,80},{20,84},{24,88},{28,92},{32,9... | collective-permute-start | bytes 1572872 | tf_op jit(solution)/shard_map/ppermute | solution.py:15
  100.3 6.1 %collective-permute-done.8 = bf16[256,1024]{1,0:T(8,128)(2,1)S(1)} collective-permute-done((bf16[256,1024]{1,0:T(8,128)(2,1)}, bf16[256,1024]{1,0:T(8,128)(2,1)S(1)}, u32[]{:S(2)}, u32[]{:S(2)}) %collective-permute-start.8) | collective-permute-done | bytes 524320 | tf_op jit(solution)/shard_map/ppermute | solution.py:15
  107.2 5.3 %gather_fusion.2 = bf16[16,128,1024]{2,1,0:T(8,128)(2,1)} fusion(bf16[20,128,1024]{2,1,0:T(8,128)(2,1)} %bitcast.311, s32[1024]{0:T(1024)S(1)} %pad_clamp_fusion.1), kind=kCustom, calls=%fused_computation.2 | custom fusion | bytes 8388672 | tf_op jit(solution)/shard_map/gather | solution.py:57
  112.5 6.4 %copy.98 = bf16[16,128,1024]{1,2,0:T(8,128)(2,1)} copy(bf16[16,128,1024]{2,1,0:T(8,128)(2,1)} %gather_fusion.2) | data formatting | bytes 8388608 | tf_op jit(solution)/shard_map/gather | solution.py:57
  134.6 5.2 %fusion.9 = f32[2,8,128,8,64]{2,4,1,3,0:T(8,128)S(1)} fusion(bf16[2,128,8,64,1]{1,0,3,2,4:T(2,128)(2,1)S(1)} %bitcast.316, f32[8,2,128,8,128]{2,4,3,1,0:T(8,128)} %copy-done.2, f32[8,2,128]{2,1,0:T(2,128)S(1)} %bitcast.351), kind=kOutput, calls=%fused_computation.31 | convolution fusion | flops 274726912 | bytes 12853248 | tf_op jit(solution)/shard_map/haikj,aihd->akjhd/dot_general | solution.py:140
  139.8 5.5 %multiply_convert_fusion = bf16[8,2,128,8,128]{2,4,3,1,0:T(8,128)(2,1)S(1)} fusion(f32[8,2,128,8,128]{2,4,3,1,0:T(8,128)} %copy-done.2, f32[8,2,128]{2,1,0:T(2,128)S(1)} %copy.131, f32[8,2,128]{2,1,0:T(2,128)S(1)} %bitcast.352, bf16[2,8,128,8,64]{2,4,3,1,0:T(8,128)(2,1)S(1)} %bitcast.322, bf16[2,128,8,64,1]{1,0,3,2,4:T(2,128)(2,1)S(1)} %bitcast.317), kind=kOutput, calls=%fused_computation.12 | convolution fusion | flops 281018368 | bytes 14958592 | tf_op jit(solution)/shard_map/aihd,akjhd->haikj/dot_general | solution.py:127
  152.0 9.3 %copy.118 = f32[16,128,1024]{2,1,0:T(8,128)} copy(f32[16,128,1024]{1,2,0:T(8,128)} %bitcast.297) | data formatting | bytes 16777216 | tf_op jit(solution)/shard_map/concatenate | solution.py:144
  161.2 5.3 %broadcast_in_dim.151 = f32[20,128,1024]{2,1,0:T(8,128)} broadcast(f32[]{:T(128)} %constant.469.clone.1), dimensions={} | broadcast | bytes 10485764 | tf_op jit(solution)/shard_map/broadcast_in_dim | solution.py:149
  166.6 18.3 %scatter_fusion = f32[20,128,1024]{2,1,0:T(8,128)} fusion(f32[20,128,1024]{2,1,0:T(8,128)} %broadcast_in_dim.151, s32[16]{0:T(128)S(1)} %reshape.628, f32[16,128,1024]{2,1,0:T(8,128)} %copy.118), kind=kCustom, calls=%fused_computation.9 | custom fusion | flops 2097152 | bytes 25165888 | tf_op jit(solution)/shard_map/scatter-add | solution.py:149
  192.0 5.1 %collective-permute-start.11 = (bf16[256,1024]{1,0:T(8,128)(2,1)}, bf16[256,1024]{1,0:T(8,128)(2,1)}, u32[]{:S(2)}, u32[]{:S(2)}) collective-permute-start(bf16[256,1024]{1,0:T(8,128)(2,1)} %bitcast.59), channel_id=1, source_target_pairs={{0,120},{4,124},{8,0},{12,4},{16,8},{20,12},{24,16},{28,20},{32,24... | collective-permute-start | bytes 1572872 | tf_op jit(solution)/shard_map/ppermute | solution.py:15
  205.4 26.0 %collective-permute-done.11 = bf16[256,1024]{1,0:T(8,128)(2,1)} collective-permute-done((bf16[256,1024]{1,0:T(8,128)(2,1)}, bf16[256,1024]{1,0:T(8,128)(2,1)}, u32[]{:S(2)}, u32[]{:S(2)}) %collective-permute-start.11) | collective-permute-done | bytes 524320 | tf_op jit(solution)/shard_map/ppermute | solution.py:15
  231.4 6.6 %collective-permute-done.12 = bf16[256,1024]{1,0:T(8,128)(2,1)} collective-permute-done((bf16[256,1024]{1,0:T(8,128)(2,1)}, bf16[256,1024]{1,0:T(8,128)(2,1)}, u32[]{:S(2)}, u32[]{:S(2)}) %collective-permute-start.12) | collective-permute-done | bytes 524320 | tf_op jit(solution)/shard_map/ppermute | solution.py:15
  249.2 11.9 %collective-permute-done.17 = bf16[256,1024]{1,0:T(8,128)(2,1)} collective-permute-done((bf16[256,1024]{1,0:T(8,128)(2,1)}, bf16[256,1024]{1,0:T(8,128)(2,1)}, u32[]{:S(2)}, u32[]{:S(2)}) %collective-permute-start.17) | collective-permute-done | bytes 524320 | tf_op jit(solution)/shard_map/ppermute | solution.py:15
  289.4 5.5 %collective-permute-done.20 = bf16[264,512]{1,0:T(8,128)(2,1)S(1)} collective-permute-done((bf16[264,512]{1,0:T(8,128)(2,1)S(1)}, bf16[264,512]{1,0:T(8,128)(2,1)S(1)}, u32[]{:S(2)}, u32[]{:S(2)}) %collective-permute-start.20) | collective-permute-done | bytes 270368 | tf_op jit(solution)/shard_map/ppermute | solution.py:175
  301.8 7.9 %all-to-all-start.1 = ((bf16[32,16,512]{2,1,0:T(8,128)(2,1)}), bf16[32,16,512]{2,1,0:T(8,128)(2,1)S(1)}, u32[]{:S(2)}, u32[]{:S(2)}) async-start(bf16[32,16,512]{2,1,0:T(8,128)(2,1)} %bitcast.38), calls=%async_computation.1 | async-start | bytes 1048576 | tf_op jit(solution)/shard_map/all_to_all | solution.py:301
  314.5 5.4 %collective-permute-done.23 = bf16[72,512]{1,0:T(8,128)(2,1)S(1)} collective-permute-done((bf16[72,512]{1,0:T(8,128)(2,1)S(1)}, bf16[72,512]{1,0:T(8,128)(2,1)S(1)}, u32[]{:S(2)}, u32[]{:S(2)}) %collective-permute-start.23) | collective-permute-done | bytes 73760 | tf_op jit(solution)/shard_map/ppermute | solution.py:175
  343.8 8.7 %all-to-all-start.3 = ((bf16[32,16,512]{2,1,0:T(8,128)(2,1)}), bf16[32,16,512]{2,1,0:T(8,128)(2,1)S(1)}, u32[]{:S(2)}, u32[]{:S(2)}) async-start(bf16[32,16,512]{2,1,0:T(8,128)(2,1)} %bitcast.66), calls=%async_computation.3 | async-start | bytes 1048576 | tf_op jit(solution)/shard_map/all_to_all | solution.py:350
  355.9 8.3 %all-to-all-done.3 = bf16[32,16,512]{2,1,0:T(8,128)(2,1)S(1)} async-done(((bf16[32,16,512]{2,1,0:T(8,128)(2,1)}), bf16[32,16,512]{2,1,0:T(8,128)(2,1)S(1)}, u32[]{:S(2)}, u32[]{:S(2)}) %all-to-all-start.3) | async-done | bytes 524320 | tf_op jit(solution)/shard_map/all_to_all | solution.py:350
  369.4 6.3 %collective-permute-done.35 = bf16[256,512]{1,0:T(8,128)(2,1)S(1)} collective-permute-done((bf16[256,512]{1,0:T(8,128)(2,1)S(1)}, bf16[256,512]{1,0:T(8,128)(2,1)S(1)}, u32[]{:S(2)}, u32[]{:S(2)}) %collective-permute-start.35) | collective-permute-done | bytes 262176 | tf_op jit(solution)/shard_map/ppermute | solution.py:175
  375.7 7.3 %collective-permute-done.36 = bf16[256,512]{1,0:T(8,128)(2,1)S(1)} collective-permute-done((bf16[256,512]{1,0:T(8,128)(2,1)S(1)}, bf16[256,512]{1,0:T(8,128)(2,1)S(1)}, u32[]{:S(2)}, u32[]{:S(2)}) %collective-permute-start.36) | collective-permute-done | bytes 262176 | tf_op jit(solution)/shard_map/ppermute | solution.py:175
  389.9 96.8 %all-reduce.4.cloned.1.call-done = (f32[512,2048]{1,0:T(8,128)}, f32[2048,512]{1,0:T(8,128)}) async-done(((f32[512,2048]{1,0:T(8,128)}, f32[2048,512]{1,0:T(8,128)}), (f32[512,2048]{1,0:T(8,128)}, f32[2048,512]{1,0:T(8,128)})) %all-reduce.4.cloned.1.call-update) | async-done | bytes 8388624 | tf_op jit(solution)/shard_map/psum | solution.py:321
  486.7 4.8 copy.262
  (295 shorter events, 189.6 us)
Async XLA Ops:
  14.5 20.1 %all-to-all-start = ((bf16[32,16,512]{2,1,0:T(8,128)(2,1)}), bf16[32,16,512]{2,1,0:T(8,128)(2,1)S(1)}, u32[]{:S(2)}, u32[]{:S(2)}) async-start(bf16[32,16,512]{2,1,0:T(8,128)(2,1)} %bitcast.16), calls=%async_computation | async-start | bytes 1048576 | tf_op jit(solution)/shard_map/all_to_all | solution.py:262
  34.6 16.2 %all-to-all-start.2 = ((bf16[32,16,512]{2,1,0:T(8,128)(2,1)}), bf16[32,16,512]{2,1,0:T(8,128)(2,1)S(1)}, u32[]{:S(2)}, u32[]{:S(2)}) async-start(bf16[32,16,512]{2,1,0:T(8,128)(2,1)} %bitcast.320), calls=%async_computation.2 | async-start | bytes 1048576 | tf_op jit(solution)/shard_map/all_to_all | solution.py:308
  45.9 17.1 %collective-permute-start.1 = (bf16[256,1024]{1,0:T(8,128)(2,1)}, bf16[256,1024]{1,0:T(8,128)(2,1)}, u32[]{:S(2)}, u32[]{:S(2)}) collective-permute-start(bf16[256,1024]{1,0:T(8,128)(2,1)} %get-tuple-element.69), channel_id=1, source_target_pairs={{0,124},{4,0},{8,4},{12,8},{16,12},{20,16},{24,20},{28,24},{32,28}... | collective-permute-start | bytes 1572872 | tf_op jit(solution)/shard_map/ppermute | solution.py:15
  45.9 23.1 %collective-permute-start.2 = (bf16[256,1024]{1,0:T(8,128)(2,1)}, bf16[256,1024]{1,0:T(8,128)(2,1)}, u32[]{:S(2)}, u32[]{:S(2)}) collective-permute-start(bf16[256,1024]{1,0:T(8,128)(2,1)} %get-tuple-element.69), channel_id=1, source_target_pairs={{0,8},{4,12},{8,16},{12,20},{16,24},{20,28},{24,32},{28,36},{32,40... | collective-permute-start | bytes 1572872 | tf_op jit(solution)/shard_map/ppermute | solution.py:15
  47.2 26.8 %collective-permute-start.3 = (bf16[256,1024]{1,0:T(8,128)(2,1)}, bf16[256,1024]{1,0:T(8,128)(2,1)}, u32[]{:S(2)}, u32[]{:S(2)}) collective-permute-start(bf16[256,1024]{1,0:T(8,128)(2,1)} %get-tuple-element.69), channel_id=1, source_target_pairs={{0,120},{4,124},{8,0},{12,4},{16,8},{20,12},{24,16},{28,20},{32,24... | collective-permute-start | bytes 1572872 | tf_op jit(solution)/shard_map/ppermute | solution.py:15
  50.8 45.0 %collective-permute-start.4 = (bf16[256,1024]{1,0:T(8,128)(2,1)}, bf16[256,1024]{1,0:T(8,128)(2,1)}, u32[]{:S(2)}, u32[]{:S(2)}) collective-permute-start(bf16[256,1024]{1,0:T(8,128)(2,1)} %get-tuple-element.69), channel_id=1, source_target_pairs={{0,16},{4,20},{8,24},{12,28},{16,32},{20,36},{24,40},{28,44},{32,4... | collective-permute-start | bytes 1572872 | tf_op jit(solution)/shard_map/ppermute | solution.py:15
  55.9 41.7 %collective-permute-start.5 = (bf16[256,1024]{1,0:T(8,128)(2,1)}, bf16[256,1024]{1,0:T(8,128)(2,1)S(1)}, u32[]{:S(2)}, u32[]{:S(2)}) collective-permute-start(bf16[256,1024]{1,0:T(8,128)(2,1)} %get-tuple-element.69), channel_id=1, source_target_pairs={{0,112},{4,116},{8,120},{12,124},{16,0},{20,4},{24,8},{28,12},{32,... | collective-permute-start | bytes 1572872 | tf_op jit(solution)/shard_map/ppermute | solution.py:15
  63.0 35.5 %collective-permute-start.6 = (bf16[256,1024]{1,0:T(8,128)(2,1)}, bf16[256,1024]{1,0:T(8,128)(2,1)S(1)}, u32[]{:S(2)}, u32[]{:S(2)}) collective-permute-start(bf16[256,1024]{1,0:T(8,128)(2,1)} %get-tuple-element.69), channel_id=1, source_target_pairs={{0,32},{4,36},{8,40},{12,44},{16,48},{20,52},{24,56},{28,60},{32,6... | collective-permute-start | bytes 1572872 | tf_op jit(solution)/shard_map/ppermute | solution.py:15
  69.0 30.5 %collective-permute-start.7 = (bf16[256,1024]{1,0:T(8,128)(2,1)}, bf16[256,1024]{1,0:T(8,128)(2,1)S(1)}, u32[]{:S(2)}, u32[]{:S(2)}) collective-permute-start(bf16[256,1024]{1,0:T(8,128)(2,1)} %get-tuple-element.69), channel_id=1, source_target_pairs={{0,96},{4,100},{8,104},{12,108},{16,112},{20,116},{24,120},{28,124... | collective-permute-start | bytes 1572872 | tf_op jit(solution)/shard_map/ppermute | solution.py:15
  73.9 32.4 %collective-permute-start.8 = (bf16[256,1024]{1,0:T(8,128)(2,1)}, bf16[256,1024]{1,0:T(8,128)(2,1)S(1)}, u32[]{:S(2)}, u32[]{:S(2)}) collective-permute-start(bf16[256,1024]{1,0:T(8,128)(2,1)} %get-tuple-element.69), channel_id=1, source_target_pairs={{0,64},{4,68},{8,72},{12,76},{16,80},{20,84},{24,88},{28,92},{32,9... | collective-permute-start | bytes 1572872 | tf_op jit(solution)/shard_map/ppermute | solution.py:15
  192.0 39.4 %collective-permute-start.11 = (bf16[256,1024]{1,0:T(8,128)(2,1)}, bf16[256,1024]{1,0:T(8,128)(2,1)}, u32[]{:S(2)}, u32[]{:S(2)}) collective-permute-start(bf16[256,1024]{1,0:T(8,128)(2,1)} %bitcast.59), channel_id=1, source_target_pairs={{0,120},{4,124},{8,0},{12,4},{16,8},{20,12},{24,16},{28,20},{32,24... | collective-permute-start | bytes 1572872 | tf_op jit(solution)/shard_map/ppermute | solution.py:15
  197.2 40.8 %collective-permute-start.12 = (bf16[256,1024]{1,0:T(8,128)(2,1)}, bf16[256,1024]{1,0:T(8,128)(2,1)}, u32[]{:S(2)}, u32[]{:S(2)}) collective-permute-start(bf16[256,1024]{1,0:T(8,128)(2,1)} %bitcast.60), channel_id=1, source_target_pairs={{0,8},{4,12},{8,16},{12,20},{16,24},{20,28},{24,32},{28,36},{32,40... | collective-permute-start | bytes 1572872 | tf_op jit(solution)/shard_map/ppermute | solution.py:15
  197.2 40.8 %collective-permute-start.13 = (bf16[256,1024]{1,0:T(8,128)(2,1)}, bf16[256,1024]{1,0:T(8,128)(2,1)}, u32[]{:S(2)}, u32[]{:S(2)}) collective-permute-start(bf16[256,1024]{1,0:T(8,128)(2,1)} %bitcast.61), channel_id=1, source_target_pairs={{0,112},{4,116},{8,120},{12,124},{16,0},{20,4},{24,8},{28,12},{32,... | collective-permute-start | bytes 1572872 | tf_op jit(solution)/shard_map/ppermute | solution.py:15
  200.7 45.6 %collective-permute-start.14 = (bf16[256,1024]{1,0:T(8,128)(2,1)}, bf16[256,1024]{1,0:T(8,128)(2,1)}, u32[]{:S(2)}, u32[]{:S(2)}) collective-permute-start(bf16[256,1024]{1,0:T(8,128)(2,1)} %bitcast.334), channel_id=1, source_target_pairs={{0,16},{4,20},{8,24},{12,28},{16,32},{20,36},{24,40},{28,44},{32,4... | collective-permute-start | bytes 1572872 | tf_op jit(solution)/shard_map/ppermute | solution.py:15
  202.4 43.9 %collective-permute-start.15 = (bf16[256,1024]{1,0:T(8,128)(2,1)}, bf16[256,1024]{1,0:T(8,128)(2,1)}, u32[]{:S(2)}, u32[]{:S(2)}) collective-permute-start(bf16[256,1024]{1,0:T(8,128)(2,1)} %bitcast.333), channel_id=1, source_target_pairs={{0,96},{4,100},{8,104},{12,108},{16,112},{20,116},{24,120},{28,124... | collective-permute-start | bytes 1572872 | tf_op jit(solution)/shard_map/ppermute | solution.py:15
  231.4 17.8 %collective-permute-start.16 = (bf16[256,1024]{1,0:T(8,128)(2,1)}, bf16[256,1024]{1,0:T(8,128)(2,1)}, u32[]{:S(2)}, u32[]{:S(2)}) collective-permute-start(bf16[256,1024]{1,0:T(8,128)(2,1)} %bitcast.332), channel_id=1, source_target_pairs={{0,32},{4,36},{8,40},{12,44},{16,48},{20,52},{24,56},{28,60},{32,6... | collective-permute-start | bytes 1572872 | tf_op jit(solution)/shard_map/ppermute | solution.py:15
  238.0 23.0 %collective-permute-start.17 = (bf16[256,1024]{1,0:T(8,128)(2,1)}, bf16[256,1024]{1,0:T(8,128)(2,1)}, u32[]{:S(2)}, u32[]{:S(2)}) collective-permute-start(bf16[256,1024]{1,0:T(8,128)(2,1)} %bitcast.331), channel_id=1, source_target_pairs={{0,64},{4,68},{8,72},{12,76},{16,80},{20,84},{24,88},{28,92},{32,9... | collective-permute-start | bytes 1572872 | tf_op jit(solution)/shard_map/ppermute | solution.py:15
  238.0 23.0 %collective-permute-start.9 = (bf16[256,1024]{1,0:T(8,128)(2,1)}, bf16[256,1024]{1,0:T(8,128)(2,1)}, u32[]{:S(2)}, u32[]{:S(2)}) collective-permute-start(bf16[256,1024]{1,0:T(8,128)(2,1)} %bitcast.330), channel_id=1, source_target_pairs={{0,124},{4,0},{8,4},{12,8},{16,12},{20,16},{24,20},{28,24},{32,28}... | collective-permute-start | bytes 1572872 | tf_op jit(solution)/shard_map/ppermute | solution.py:15
  296.2 18.3 %collective-permute-start.22 = (bf16[72,512]{1,0:T(8,128)(2,1)}, bf16[72,512]{1,0:T(8,128)(2,1)S(1)}, u32[]{:S(2)}, u32[]{:S(2)}) collective-permute-start(bf16[72,512]{1,0:T(8,128)(2,1)} %get-tuple-element.84), channel_id=1, source_target_pairs={{0,32},{4,36},{8,40},{12,44},{16,48},{20,52},{24,56},{28,60},{32,6... | collective-permute-start | bytes 221192 | tf_op jit(solution)/shard_map/ppermute | solution.py:175
  301.8 42.0 %all-to-all-start.1 = ((bf16[32,16,512]{2,1,0:T(8,128)(2,1)}), bf16[32,16,512]{2,1,0:T(8,128)(2,1)S(1)}, u32[]{:S(2)}, u32[]{:S(2)}) async-start(bf16[32,16,512]{2,1,0:T(8,128)(2,1)} %bitcast.38), calls=%async_computation.1 | async-start | bytes 1048576 | tf_op jit(solution)/shard_map/all_to_all | solution.py:301
  309.7 177.0 %all-reduce.4.cloned.1.call-start = ((), (), s32[]{:S(2)}) async-start(), calls=%async_computation.4 | async-start | bytes 16777216 | tf_op jit(solution)/shard_map/psum | solution.py:321
  343.8 20.4 %all-to-all-start.3 = ((bf16[32,16,512]{2,1,0:T(8,128)(2,1)}), bf16[32,16,512]{2,1,0:T(8,128)(2,1)S(1)}, u32[]{:S(2)}, u32[]{:S(2)}) async-start(bf16[32,16,512]{2,1,0:T(8,128)(2,1)} %bitcast.66), calls=%async_computation.3 | async-start | bytes 1048576 | tf_op jit(solution)/shard_map/all_to_all | solution.py:350
  352.6 16.7 %collective-permute-start.34 = (bf16[256,512]{1,0:T(8,128)(2,1)S(1)}, bf16[256,512]{1,0:T(8,128)(2,1)S(1)}, u32[]{:S(2)}, u32[]{:S(2)}) collective-permute-start(bf16[256,512]{1,0:T(8,128)(2,1)S(1)} %bitcast.326), channel_id=1, source_target_pairs={{0,8},{4,12},{8,16},{12,20},{16,24},{20,28},{24,0},{28,4},{32,40},... | collective-permute-start | bytes 786440 | tf_op jit(solution)/shard_map/ppermute | solution.py:175
  367.0 16.0 %collective-permute-start.36 = (bf16[256,512]{1,0:T(8,128)(2,1)S(1)}, bf16[256,512]{1,0:T(8,128)(2,1)S(1)}, u32[]{:S(2)}, u32[]{:S(2)}) collective-permute-start(bf16[256,512]{1,0:T(8,128)(2,1)S(1)} %bitcast.328), channel_id=1, source_target_pairs={{0,24},{4,28},{8,0},{12,4},{16,8},{20,12},{24,16},{28,20},{32,56},... | collective-permute-start | bytes 786440 | tf_op jit(solution)/shard_map/ppermute | solution.py:175
  (52 other events, 566.6 us)
Sparse Core Ops, SparseCore 0:
  316.4 170.2 all-reduce.3
where the time goes:
time: 511 us; the launch traced here: 501 us
  waiting for transfers between devices  205 us (40%)
  starting transfers between devices  102 us (20%)
  local copies, waits for them, and re-layouts  86.5 us (17%)
  other arithmetic  50 us (10%)
  matrix products  42.6 us (8%)
  between operations  15.3 us (3%)
    psum x1, waiting for transfers between devices, on_device(): grad_up, grad_down = lax.psum((grad_up, grad_down), ('seq', 'dp'))  96.8 us
    ppermute x18, waiting for transfers between devices, from_behind(): lax.ppermute(x, axis, [(i, (i + by) % length) for i in range(length)])  57.8 us
    ppermute x18, starting transfers between devices, from_behind(): lax.ppermute(x, axis, [(i, (i + by) % length) for i in range(length)])  46.6 us
    ppermute x12, waiting for transfers between devices, ring_send(): return lax.ppermute(rows, 'seq', [(i, move(i)) for i in range(size)])  31.1 us
    unnamed x74, local copies, waits for them, and re-layouts  25.1 us
    scatter-add x1, other arithmetic, attention_backward(): jnp.zeros((total_rows // BLK, BLK, 2 * D), jnp.float32).at[selected]  18.3 us
    ppermute x12, starting transfers between devices, ring_send(): return lax.ppermute(rows, 'seq', [(i, move(i)) for i in range(size)])  15.9 us
    gather x2, local copies, waits for them, and re-layouts, listed_heads(): picked = blocks[selected]  11.7 us
  transfers between devices with their start and end apart: 43, of which 23 were waited for; matrix products, arithmetic and copies ran while one was open for 13% of the time, Pallas kernels for 0%

commit v1 on v0

--- a/solution.py
+++ b/solution.py
@@ -8,6 +8,11 @@
 HEADS = 8
 BLK = 128
 EPSILON = 1e-05
+
+
+def by_each_axis(array, inner_axis, outer_axis):
+    partial_2 = lax.psum(array, inner_axis)
+    return lax.psum(partial_2, outer_axis)
 
 
 def from_behind(x, axis, by):
@@ -318,7 +323,7 @@
     grad_normed_b = times_transposed(grad_pre, w_up)
     grad_up = inner_rows(normed_b, grad_pre)
     grad_gain2 = jnp.sum(grad_normed_b * normed2, axis=0)
-    grad_up, grad_down = lax.psum((grad_up, grad_down), ("seq", "dp"))
+    grad_up, grad_down = by_each_axis((grad_up, grad_down), "seq", "dp")
     grad_hidden = (
         grad_curve.astype(jnp.float32) + norm_back(grad_normed_b, ln2_gain, normed2, inverse2)
     ).astype(jnp.bfloat16)

time: 511 us -> 569 us (1.11)
  waiting for transfers between devices: 205 us -> 256 us
  local copies, waits for them, and re-layouts: 86.5 us -> 93.4 us
    psum x1 -> x2, waiting for transfers between devices: 96.8 us -> 147 us  [the longest x1 77.5 us: by_each_axis(): partial_2 = lax.psum(array, inner_axis)]
    unnamed x74 -> x82, local copies, waits for them, and re-layouts: 25.1 us -> 29.6 us
  transfers between devices with their start and end apart: 43 -> 44, of which waited for: 23 -> 24; matrix products, arithmetic and copies ran while one was open for 13% -> 14% of each run, Pallas kernels for 0% -> 0%
where the time goes in v1:
time: 569 us; the launch traced here: 559 us
  waiting for transfers between devices  256 us (45%)
  starting transfers between devices  98.9 us (17%)
  local copies, waits for them, and re-layouts  93.4 us (16%)
  other arithmetic  53.4 us (9%)
  matrix products  41.2 us (7%)
  between operations  15.3 us (3%)
    psum x1, waiting for transfers between devices, by_each_axis(): partial_2 = lax.psum(array, inner_axis)  77.5 us
    psum x1, waiting for transfers between devices, by_each_axis(): return lax.psum(partial_2, outer_axis)  69.1 us
    ppermute x18, waiting for transfers between devices, from_behind(): lax.ppermute(x, axis, [(i, (i + by) % length) for i in range(length)])  56.6 us
    ppermute x18, starting transfers between devices, from_behind(): lax.ppermute(x, axis, [(i, (i + by) % length) for i in range(length)])  44.1 us
    ppermute x12, waiting for transfers between devices, ring_send(): return lax.ppermute(rows, 'seq', [(i, move(i)) for i in range(size)])  31.5 us
    unnamed x82, local copies, waits for them, and re-layouts  29.6 us
    scatter-add x1, other arithmetic, attention_backward(): jnp.zeros((total_rows // BLK, BLK, 2 * D), jnp.float32).at[selected]  18.4 us
    ppermute x12, starting transfers between devices, ring_send(): return lax.ppermute(rows, 'seq', [(i, move(i)) for i in range(size)])  15.9 us
  transfers between devices with their start and end apart: 44, of which 24 were waited for; matrix products, arithmetic and copies ran while one was open for 14% of the time, Pallas kernels for 0%

profile of v1, /device:TPU:1, one launch (start us, length us, event | category | flops | bytes accessed | tf_op | source)
XLA Modules:
  0.0 558.7 jit_solution(3144665921816767872)
XLA Ops:
  14.5 8.6 %all-to-all-start = ((bf16[32,16,512]{2,1,0:T(8,128)(2,1)}), bf16[32,16,512]{2,1,0:T(8,128)(2,1)S(1)}, u32[]{:S(2)}, u32[]{:S(2)}) async-start(bf16[32,16,512]{2,1,0:T(8,128)(2,1)} %bitcast.16), calls=%async_computation | async-start | bytes 1048576 | tf_op jit(solution)/shard_map/all_to_all | solution.py:267
  56.0 5.1 collective-permute-start.5
  74.1 19.8 %collective-permute-start.8 = (bf16[256,1024]{1,0:T(8,128)(2,1)}, bf16[256,1024]{1,0:T(8,128)(2,1)S(1)}, u32[]{:S(2)}, u32[]{:S(2)}) collective-permute-start(bf16[256,1024]{1,0:T(8,128)(2,1)} %get-tuple-element.71), channel_id=1, source_target_pairs={{0,64},{4,68},{8,72},{12,76},{16,80},{20,84},{24,88},{28,92},{32,9... | collective-permute-start | bytes 1572872 | tf_op jit(solution)/shard_map/ppermute | solution.py:20
  100.8 5.7 %collective-permute-done.8 = bf16[256,1024]{1,0:T(8,128)(2,1)S(1)} collective-permute-done((bf16[256,1024]{1,0:T(8,128)(2,1)}, bf16[256,1024]{1,0:T(8,128)(2,1)S(1)}, u32[]{:S(2)}, u32[]{:S(2)}) %collective-permute-start.8) | collective-permute-done | bytes 524320 | tf_op jit(solution)/shard_map/ppermute | solution.py:20
  107.4 5.3 gather_fusion.2
  112.7 6.4 %copy.98 = bf16[16,128,1024]{1,2,0:T(8,128)(2,1)} copy(bf16[16,128,1024]{2,1,0:T(8,128)(2,1)} %gather_fusion.2) | data formatting | bytes 8388608 | tf_op jit(solution)/shard_map/gather | solution.py:62
  134.8 5.2 fusion.9
  140.0 5.4 multiply_convert_fusion
  152.1 9.3 %copy.118 = f32[16,128,1024]{2,1,0:T(8,128)} copy(f32[16,128,1024]{1,2,0:T(8,128)} %bitcast.297) | data formatting | bytes 16777216 | tf_op jit(solution)/shard_map/concatenate | solution.py:149
  161.4 5.3 broadcast_in_dim.151
  166.8 18.4 %scatter_fusion = f32[20,128,1024]{2,1,0:T(8,128)} fusion(f32[20,128,1024]{2,1,0:T(8,128)} %broadcast_in_dim.151, s32[16]{0:T(128)S(1)} %reshape.628, f32[16,128,1024]{2,1,0:T(8,128)} %copy.118), kind=kCustom, calls=%fused_computation.9 | custom fusion | flops 2097152 | bytes 25165888 | tf_op jit(solution)/shard_map/scatter-add | solution.py:154
  212.1 19.5 %collective-permute-done.11 = bf16[256,1024]{1,0:T(8,128)(2,1)} collective-permute-done((bf16[256,1024]{1,0:T(8,128)(2,1)}, bf16[256,1024]{1,0:T(8,128)(2,1)}, u32[]{:S(2)}, u32[]{:S(2)}) %collective-permute-start.11) | collective-permute-done | bytes 524320 | tf_op jit(solution)/shard_map/ppermute | solution.py:20
  231.6 6.6 %collective-permute-done.12 = bf16[256,1024]{1,0:T(8,128)(2,1)} collective-permute-done((bf16[256,1024]{1,0:T(8,128)(2,1)}, bf16[256,1024]{1,0:T(8,128)(2,1)}, u32[]{:S(2)}, u32[]{:S(2)}) %collective-permute-start.12) | collective-permute-done | bytes 524320 | tf_op jit(solution)/shard_map/ppermute | solution.py:20
  244.2 5.2 collective-permute-done.16
  249.4 14.7 %collective-permute-done.17 = bf16[256,1024]{1,0:T(8,128)(2,1)} collective-permute-done((bf16[256,1024]{1,0:T(8,128)(2,1)}, bf16[256,1024]{1,0:T(8,128)(2,1)}, u32[]{:S(2)}, u32[]{:S(2)}) %collective-permute-start.17) | collective-permute-done | bytes 524320 | tf_op jit(solution)/shard_map/ppermute | solution.py:20
  288.4 6.4 %collective-permute-done.19 = bf16[264,512]{1,0:T(8,128)(2,1)} collective-permute-done((bf16[264,512]{1,0:T(8,128)(2,1)}, bf16[264,512]{1,0:T(8,128)(2,1)}, u32[]{:S(2)}, u32[]{:S(2)}) %collective-permute-start.19) | collective-permute-done | bytes 270368 | tf_op jit(solution)/shard_map/ppermute | solution.py:180
  295.4 5.4 collective-permute-done.20
  302.2 77.5 %all-reduce.6.cloned.1.call-done = (f32[512,2048]{1,0:T(8,128)}, f32[2048,512]{1,0:T(8,128)}) async-done(((f32[512,2048]{1,0:T(8,128)}, f32[2048,512]{1,0:T(8,128)}), (f32[512,2048]{1,0:T(8,128)}, f32[2048,512]{1,0:T(8,128)})) %all-reduce.6.cloned.1.call-update) | async-done | bytes 8388624 | tf_op jit(solution)/shard_map/psum | solution.py:14
  389.5 7.4 %all-to-all-start.1 = ((bf16[32,16,512]{2,1,0:T(8,128)(2,1)}), bf16[32,16,512]{2,1,0:T(8,128)(2,1)S(1)}, u32[]{:S(2)}, u32[]{:S(2)}) async-start(bf16[32,16,512]{2,1,0:T(8,128)(2,1)} %bitcast.38), calls=%async_computation.1 | async-start | bytes 1048576 | tf_op jit(solution)/shard_map/all_to_all | solution.py:306
  400.7 6.3 %collective-permute-done.23 = bf16[72,512]{1,0:T(8,128)(2,1)S(1)} collective-permute-done((bf16[72,512]{1,0:T(8,128)(2,1)S(1)}, bf16[72,512]{1,0:T(8,128)(2,1)S(1)}, u32[]{:S(2)}, u32[]{:S(2)}) %collective-permute-start.23) | collective-permute-done | bytes 73760 | tf_op jit(solution)/shard_map/ppermute | solution.py:180
  432.5 8.6 %all-to-all-start.3 = ((bf16[32,16,512]{2,1,0:T(8,128)(2,1)}), bf16[32,16,512]{2,1,0:T(8,128)(2,1)S(1)}, u32[]{:S(2)}, u32[]{:S(2)}) async-start(bf16[32,16,512]{2,1,0:T(8,128)(2,1)} %bitcast.66), calls=%async_computation.3 | async-start | bytes 1048576 | tf_op jit(solution)/shard_map/all_to_all | solution.py:355
  444.5 8.3 %all-to-all-done.3 = bf16[32,16,512]{2,1,0:T(8,128)(2,1)S(1)} async-done(((bf16[32,16,512]{2,1,0:T(8,128)(2,1)}), bf16[32,16,512]{2,1,0:T(8,128)(2,1)S(1)}, u32[]{:S(2)}, u32[]{:S(2)}) %all-to-all-start.3) | async-done | bytes 524320 | tf_op jit(solution)/shard_map/all_to_all | solution.py:355
  457.6 6.1 %collective-permute-done.35 = bf16[256,512]{1,0:T(8,128)(2,1)S(1)} collective-permute-done((bf16[256,512]{1,0:T(8,128)(2,1)S(1)}, bf16[256,512]{1,0:T(8,128)(2,1)S(1)}, u32[]{:S(2)}, u32[]{:S(2)}) %collective-permute-start.35) | collective-permute-done | bytes 262176 | tf_op jit(solution)/shard_map/ppermute | solution.py:180
  475.7 69.1 %all-reduce.8.cloned.1.call-done = (f32[512,2048]{1,0:T(8,128)}, f32[2048,512]{1,0:T(8,128)}) async-done(((f32[512,2048]{1,0:T(8,128)}, f32[2048,512]{1,0:T(8,128)}), (f32[512,2048]{1,0:T(8,128)}, f32[2048,512]{1,0:T(8,128)})) %all-reduce.8.cloned.1.call-update) | async-done | bytes 8388624 | tf_op jit(solution)/shard_map/psum | solution.py:15
  (306 shorter events, 207.8 us)
Async XLA Ops:
  14.5 20.1 %all-to-all-start = ((bf16[32,16,512]{2,1,0:T(8,128)(2,1)}), bf16[32,16,512]{2,1,0:T(8,128)(2,1)S(1)}, u32[]{:S(2)}, u32[]{:S(2)}) async-start(bf16[32,16,512]{2,1,0:T(8,128)(2,1)} %bitcast.16), calls=%async_computation | async-start | bytes 1048576 | tf_op jit(solution)/shard_map/all_to_all | solution.py:267
  38.6 341.1 %all-reduce.6.cloned.1.call-start = ((), (), s32[]{:S(2)}) async-start(), calls=%async_computation.4 | async-start | bytes 16777216 | tf_op jit(solution)/shard_map/psum | solution.py:14
  45.9 17.1 %collective-permute-start.1 = (bf16[256,1024]{1,0:T(8,128)(2,1)}, bf16[256,1024]{1,0:T(8,128)(2,1)}, u32[]{:S(2)}, u32[]{:S(2)}) collective-permute-start(bf16[256,1024]{1,0:T(8,128)(2,1)} %get-tuple-element.71), channel_id=1, source_target_pairs={{0,124},{4,0},{8,4},{12,8},{16,12},{20,16},{24,20},{28,24},{32,28}... | collective-permute-start | bytes 1572872 | tf_op jit(solution)/shard_map/ppermute | solution.py:20
  45.9 23.1 %collective-permute-start.2 = (bf16[256,1024]{1,0:T(8,128)(2,1)}, bf16[256,1024]{1,0:T(8,128)(2,1)}, u32[]{:S(2)}, u32[]{:S(2)}) collective-permute-start(bf16[256,1024]{1,0:T(8,128)(2,1)} %get-tuple-element.71), channel_id=1, source_target_pairs={{0,8},{4,12},{8,16},{12,20},{16,24},{20,28},{24,32},{28,36},{32,40... | collective-permute-start | bytes 1572872 | tf_op jit(solution)/shard_map/ppermute | solution.py:20
  47.2 26.9 %collective-permute-start.3 = (bf16[256,1024]{1,0:T(8,128)(2,1)}, bf16[256,1024]{1,0:T(8,128)(2,1)}, u32[]{:S(2)}, u32[]{:S(2)}) collective-permute-start(bf16[256,1024]{1,0:T(8,128)(2,1)} %get-tuple-element.71), channel_id=1, source_target_pairs={{0,120},{4,124},{8,0},{12,4},{16,8},{20,12},{24,16},{28,20},{32,24... | collective-permute-start | bytes 1572872 | tf_op jit(solution)/shard_map/ppermute | solution.py:20
  50.8 45.0 %collective-permute-start.4 = (bf16[256,1024]{1,0:T(8,128)(2,1)}, bf16[256,1024]{1,0:T(8,128)(2,1)}, u32[]{:S(2)}, u32[]{:S(2)}) collective-permute-start(bf16[256,1024]{1,0:T(8,128)(2,1)} %get-tuple-element.71), channel_id=1, source_target_pairs={{0,16},{4,20},{8,24},{12,28},{16,32},{20,36},{24,40},{28,44},{32,4... | collective-permute-start | bytes 1572872 | tf_op jit(solution)/shard_map/ppermute | solution.py:20
  56.0 41.7 %collective-permute-start.5 = (bf16[256,1024]{1,0:T(8,128)(2,1)}, bf16[256,1024]{1,0:T(8,128)(2,1)S(1)}, u32[]{:S(2)}, u32[]{:S(2)}) collective-permute-start(bf16[256,1024]{1,0:T(8,128)(2,1)} %get-tuple-element.71), channel_id=1, source_target_pairs={{0,112},{4,116},{8,120},{12,124},{16,0},{20,4},{24,8},{28,12},{32,... | collective-permute-start | bytes 1572872 | tf_op jit(solution)/shard_map/ppermute | solution.py:20
  63.0 35.5 %collective-permute-start.6 = (bf16[256,1024]{1,0:T(8,128)(2,1)}, bf16[256,1024]{1,0:T(8,128)(2,1)S(1)}, u32[]{:S(2)}, u32[]{:S(2)}) collective-permute-start(bf16[256,1024]{1,0:T(8,128)(2,1)} %get-tuple-element.71), channel_id=1, source_target_pairs={{0,32},{4,36},{8,40},{12,44},{16,48},{20,52},{24,56},{28,60},{32,6... | collective-permute-start | bytes 1572872 | tf_op jit(solution)/shard_map/ppermute | solution.py:20
  69.0 30.9 %collective-permute-start.7 = (bf16[256,1024]{1,0:T(8,128)(2,1)}, bf16[256,1024]{1,0:T(8,128)(2,1)S(1)}, u32[]{:S(2)}, u32[]{:S(2)}) collective-permute-start(bf16[256,1024]{1,0:T(8,128)(2,1)} %get-tuple-element.71), channel_id=1, source_target_pairs={{0,96},{4,100},{8,104},{12,108},{16,112},{20,116},{24,120},{28,124... | collective-permute-start | bytes 1572872 | tf_op jit(solution)/shard_map/ppermute | solution.py:20
  74.1 32.4 %collective-permute-start.8 = (bf16[256,1024]{1,0:T(8,128)(2,1)}, bf16[256,1024]{1,0:T(8,128)(2,1)S(1)}, u32[]{:S(2)}, u32[]{:S(2)}) collective-permute-start(bf16[256,1024]{1,0:T(8,128)(2,1)} %get-tuple-element.71), channel_id=1, source_target_pairs={{0,64},{4,68},{8,72},{12,76},{16,80},{20,84},{24,88},{28,92},{32,9... | collective-permute-start | bytes 1572872 | tf_op jit(solution)/shard_map/ppermute | solution.py:20
  192.4 19.1 %collective-permute-start.10 = (bf16[256,1024]{1,0:T(8,128)(2,1)}, bf16[256,1024]{1,0:T(8,128)(2,1)}, u32[]{:S(2)}, u32[]{:S(2)}) collective-permute-start(bf16[256,1024]{1,0:T(8,128)(2,1)} %bitcast.58), channel_id=1, source_target_pairs={{0,4},{4,8},{8,12},{12,16},{16,20},{20,24},{24,28},{28,32},{32,36}... | collective-permute-start | bytes 1572872 | tf_op jit(solution)/shard_map/ppermute | solution.py:20
  192.4 39.2 %collective-permute-start.11 = (bf16[256,1024]{1,0:T(8,128)(2,1)}, bf16[256,1024]{1,0:T(8,128)(2,1)}, u32[]{:S(2)}, u32[]{:S(2)}) collective-permute-start(bf16[256,1024]{1,0:T(8,128)(2,1)} %bitcast.59), channel_id=1, source_target_pairs={{0,120},{4,124},{8,0},{12,4},{16,8},{20,12},{24,16},{28,20},{32,24... | collective-permute-start | bytes 1572872 | tf_op jit(solution)/shard_map/ppermute | solution.py:20
  197.4 40.8 %collective-permute-start.12 = (bf16[256,1024]{1,0:T(8,128)(2,1)}, bf16[256,1024]{1,0:T(8,128)(2,1)}, u32[]{:S(2)}, u32[]{:S(2)}) collective-permute-start(bf16[256,1024]{1,0:T(8,128)(2,1)} %bitcast.60), channel_id=1, source_target_pairs={{0,8},{4,12},{8,16},{12,20},{16,24},{20,28},{24,32},{28,36},{32,40... | collective-permute-start | bytes 1572872 | tf_op jit(solution)/shard_map/ppermute | solution.py:20
  197.4 40.8 %collective-permute-start.13 = (bf16[256,1024]{1,0:T(8,128)(2,1)}, bf16[256,1024]{1,0:T(8,128)(2,1)}, u32[]{:S(2)}, u32[]{:S(2)}) collective-permute-start(bf16[256,1024]{1,0:T(8,128)(2,1)} %bitcast.61), channel_id=1, source_target_pairs={{0,112},{4,116},{8,120},{12,124},{16,0},{20,4},{24,8},{28,12},{32,... | collective-permute-start | bytes 1572872 | tf_op jit(solution)/shard_map/ppermute | solution.py:20
  206.8 37.5 %collective-permute-start.14 = (bf16[256,1024]{1,0:T(8,128)(2,1)}, bf16[256,1024]{1,0:T(8,128)(2,1)}, u32[]{:S(2)}, u32[]{:S(2)}) collective-permute-start(bf16[256,1024]{1,0:T(8,128)(2,1)} %bitcast.330), channel_id=1, source_target_pairs={{0,16},{4,20},{8,24},{12,28},{16,32},{20,36},{24,40},{28,44},{32,4... | collective-permute-start | bytes 1572872 | tf_op jit(solution)/shard_map/ppermute | solution.py:20
  211.5 32.8 %collective-permute-start.15 = (bf16[256,1024]{1,0:T(8,128)(2,1)}, bf16[256,1024]{1,0:T(8,128)(2,1)}, u32[]{:S(2)}, u32[]{:S(2)}) collective-permute-start(bf16[256,1024]{1,0:T(8,128)(2,1)} %bitcast.63), channel_id=1, source_target_pairs={{0,96},{4,100},{8,104},{12,108},{16,112},{20,116},{24,120},{28,124... | collective-permute-start | bytes 1572872 | tf_op jit(solution)/shard_map/ppermute | solution.py:20
  231.6 17.8 %collective-permute-start.16 = (bf16[256,1024]{1,0:T(8,128)(2,1)}, bf16[256,1024]{1,0:T(8,128)(2,1)}, u32[]{:S(2)}, u32[]{:S(2)}) collective-permute-start(bf16[256,1024]{1,0:T(8,128)(2,1)} %bitcast.64), channel_id=1, source_target_pairs={{0,32},{4,36},{8,40},{12,44},{16,48},{20,52},{24,56},{28,60},{32,6... | collective-permute-start | bytes 1572872 | tf_op jit(solution)/shard_map/ppermute | solution.py:20
  238.2 25.9 %collective-permute-start.17 = (bf16[256,1024]{1,0:T(8,128)(2,1)}, bf16[256,1024]{1,0:T(8,128)(2,1)}, u32[]{:S(2)}, u32[]{:S(2)}) collective-permute-start(bf16[256,1024]{1,0:T(8,128)(2,1)} %bitcast.65), channel_id=1, source_target_pairs={{0,64},{4,68},{8,72},{12,76},{16,80},{20,84},{24,88},{28,92},{32,9... | collective-permute-start | bytes 1572872 | tf_op jit(solution)/shard_map/ppermute | solution.py:20
  238.2 25.9 %collective-permute-start.9 = (bf16[256,1024]{1,0:T(8,128)(2,1)}, bf16[256,1024]{1,0:T(8,128)(2,1)}, u32[]{:S(2)}, u32[]{:S(2)}) collective-permute-start(bf16[256,1024]{1,0:T(8,128)(2,1)} %bitcast.57), channel_id=1, source_target_pairs={{0,124},{4,0},{8,4},{12,8},{16,12},{20,16},{24,20},{28,24},{32,28}... | collective-permute-start | bytes 1572872 | tf_op jit(solution)/shard_map/ppermute | solution.py:20
  242.0 302.8 %all-reduce.8.cloned.1.call-start = ((), (), s32[]{:S(2)}) async-start(), calls=%async_computation.5 | async-start | bytes 16777216 | tf_op jit(solution)/shard_map/psum | solution.py:15
  382.7 18.0 %collective-permute-start.22 = (bf16[72,512]{1,0:T(8,128)(2,1)}, bf16[72,512]{1,0:T(8,128)(2,1)S(1)}, u32[]{:S(2)}, u32[]{:S(2)}) collective-permute-start(bf16[72,512]{1,0:T(8,128)(2,1)} %get-tuple-element.86), channel_id=1, source_target_pairs={{0,32},{4,36},{8,40},{12,44},{16,48},{20,52},{24,56},{28,60},{32,6... | collective-permute-start | bytes 221192 | tf_op jit(solution)/shard_map/ppermute | solution.py:180
  389.5 43.0 %all-to-all-start.1 = ((bf16[32,16,512]{2,1,0:T(8,128)(2,1)}), bf16[32,16,512]{2,1,0:T(8,128)(2,1)S(1)}, u32[]{:S(2)}, u32[]{:S(2)}) async-start(bf16[32,16,512]{2,1,0:T(8,128)(2,1)} %bitcast.38), calls=%async_computation.1 | async-start | bytes 1048576 | tf_op jit(solution)/shard_map/all_to_all | solution.py:306
  432.5 20.3 %all-to-all-start.3 = ((bf16[32,16,512]{2,1,0:T(8,128)(2,1)}), bf16[32,16,512]{2,1,0:T(8,128)(2,1)S(1)}, u32[]{:S(2)}, u32[]{:S(2)}) async-start(bf16[32,16,512]{2,1,0:T(8,128)(2,1)} %bitcast.66), calls=%async_computation.3 | async-start | bytes 1048576 | tf_op jit(solution)/shard_map/all_to_all | solution.py:355
  441.2 16.4 %collective-permute-start.34 = (bf16[256,512]{1,0:T(8,128)(2,1)S(1)}, bf16[256,512]{1,0:T(8,128)(2,1)S(1)}, u32[]{:S(2)}, u32[]{:S(2)}) collective-permute-start(bf16[256,512]{1,0:T(8,128)(2,1)S(1)} %bitcast.326), channel_id=1, source_target_pairs={{0,8},{4,12},{8,16},{12,20},{16,24},{20,28},{24,0},{28,4},{32,40},... | collective-permute-start | bytes 786440 | tf_op jit(solution)/shard_map/ppermute | solution.py:180
  (57 other events, 589.0 us)
Sparse Core Ops, SparseCore 0:
  242.2 137.5 all-reduce.5
  382.5 162.2 all-reduce.7
